TPU v7x, 768 devices: a whole 4x8x12 slice. The times are simulated.
768 devices in a mesh: elem: 128 (over x, y, z_hi, core), state: 6 (over z_lo).
Axes of the slice: x: 4, y: 8, z: 12 (z_hi: 2, z_lo: 6; z = z_hi * 6 + z_lo), core: 2. Of those that a mesh axis runs over, the one named last changes fastest.
Arguments:
- orbitals: bfloat16 [1536, 160, 768], P(('elem', 'state')), may hold values from -6 to 6
- rotation: bfloat16 [768, 768], replicated, may hold values from -0.21875 to 0.21875
- counts: int32 [1536], P('elem'), may hold values from 96 to 160, as said below
- neighbors: int32 [1536, 5], P('elem'), may hold values from 0 to 1535, as said below
- blocks: bfloat16 [1536, 5, 160, 160], P('elem'), may hold values from -0.21875 to 0.21875
Outputs:
- filtered: bfloat16 [1536, 160, 768], P(('elem', 'state'))
Inputs may be any that keep to these rules, and one draw needn't show every extreme that they name: `neighbors`: entry 0 of row e is e; every other entry is (e + d) mod 1536 with 1 <= |d| <= 4. The adaptive basis is sized per pair of neighbouring elements: over each aligned block of 2 elements the counts sum to at most 288, and the first block of every index of elem sums to exactly 288.
All inputs are finite; a program needn't handle non-finite values.
Results may differ from a plain program's by a relative error of at most 0.007.
Values may be sent and summed in bfloat16 or wider, within the bound.
A program may use at most 64 MiB of HBM per device.

v0:
```python
import jax
import jax.numpy as jnp
from jax import lax
from jax.sharding import PartitionSpec as P

DEG = 4


center_shift = 0.2
half_span = 1.1


def with_halo(block, sides, width):
    for axis, dim in sides:
        count = lax.axis_size(axis)
        forward = [(i, i + 1) for i in range(count - 1)]
        forward.append((count - 1, 0))
        backward = [(target, source) for source, target in forward]
        low = lax.ppermute(
            lax.slice_in_dim(block, block.shape[dim] - width, None, axis=dim), axis, forward
        )
        high = lax.ppermute(lax.slice_in_dim(block, 0, width, axis=dim), axis, backward)
        block = jnp.concatenate([low, block, high], axis=dim)
    return block


def padded_rim(current, reach):
    return with_halo(current, (("elem", 0),), reach)


def coupled(block_part, gathered):
    return jnp.einsum("ekij,ekjs->eis", block_part, gathered, preferred_element_type=jnp.float32)


def on_device(orbitals, rotation, counts, neighbors, blocks):
    row_elems = orbitals.shape[0]
    basis_len = orbitals.shape[1]
    elems = counts.shape[0]
    reach = elems // 3
    shard = lax.axis_index("state")
    my_counts = lax.dynamic_slice_in_dim(counts, shard * row_elems, row_elems, 0)
    flat_orbitals = orbitals.reshape(row_elems * basis_len, -1)
    rows_mask = (
        lax.broadcasted_iota(jnp.int32, (row_elems, basis_len, 1), 1) < my_counts[:, None, None]
    ).astype(jnp.float32)
    rotated = jnp.dot(flat_orbitals, rotation, preferred_element_type=jnp.float32)
    rotated = rotated.reshape(row_elems, basis_len, -1)
    start_rows = (rotated * rows_mask).astype(jnp.bfloat16)
    start = lax.all_to_all(start_rows, "state", split_axis=2, concat_axis=0, tiled=True)
    elem_mask = (
        lax.broadcasted_iota(jnp.int32, (elems, basis_len, 1), 1) < counts[:, None, None]
    ).astype(jnp.float32)
    all_elems = elems * lax.axis_size("elem")
    first_global = lax.axis_index("elem") * elems
    local_source = jnp.mod(neighbors - first_global + reach, all_elems)

    def image_of(current):
        padded = padded_rim(current, reach)
        image = coupled(blocks, padded[local_source])
        return image * elem_mask

    def chebyshev(current, previous, factor, with_prev):
        value = (
            factor * (image_of(current) - center_shift * current.astype(jnp.float32)) / half_span
        )
        if with_prev:
            value = value - previous.astype(jnp.float32)
        return value.astype(jnp.bfloat16)

    previous = start
    current = chebyshev(start, start, 1.0, False)
    for degree in range(DEG - 1):
        following = chebyshev(current, previous, 2.0, True)
        previous = current
        current = following
    return lax.all_to_all(current, "state", split_axis=0, concat_axis=2, tiled=True)


def solution(mesh):
    in_specs = (
        P(("elem", "state"), None, None),
        P(),
        P("elem"),
        P("elem", None),
        P("elem", None, None, None),
    )
    out_specs = P(("elem", "state"), None, None)
    return jax.shard_map(
        on_device, mesh=mesh, in_specs=in_specs, out_specs=out_specs, check_vma=False
    )
```

profile of v0, /device:TPU:64, one launch (start us, length us, event | category | flops | bytes accessed | tf_op | source)
XLA Modules:
  0.0 196.6 jit_solution(10548008125839667392)
XLA Ops:
  0.0 0.0 copy-start
  0.0 0.8 dynamic_slice.3
  0.8 0.1 compare_convert_fusion
  0.9 0.4 copy-done
  1.3 0.0 copy-start.2
  1.3 1.6 fusion.23
  2.9 1.8 copy.16
  4.7 12.3 %all-to-all-start = ((bf16[2,160,768]{1,0,2:T(2,128)(2,1)}), bf16[2,160,768]{1,0,2:T(2,128)(2,1)S(1)}, u32[]{:S(2)}, u32[]{:S(2)}) async-start(bf16[2,160,768]{1,0,2:T(2,128)(2,1)} %copy.16), calls=%async_computation | async-start | bytes 1572864 | tf_op jit(solution)/shard_map/all_to_all | solution.py:49
  17.0 0.0 copy-done.2
  17.0 0.1 fusion.25
  17.0 22.2 %all-to-all-done = bf16[2,160,768]{1,0,2:T(2,128)(2,1)S(1)} async-done(((bf16[2,160,768]{1,0,2:T(2,128)(2,1)}), bf16[2,160,768]{1,0,2:T(2,128)(2,1)S(1)}, u32[]{:S(2)}, u32[]{:S(2)}) %all-to-all-start) | async-done | bytes 491552 | tf_op jit(solution)/shard_map/all_to_all | solution.py:49
  39.3 1.4 copy.27
  40.6 0.2 fusion.26
  40.9 13.7 %collective-permute-start.1 = (bf16[4,160,128]{2,1,0:T(8,128)(2,1)S(1)}, bf16[4,160,128]{2,1,0:T(8,128)(2,1)S(1)}, u32[]{:S(2)}, u32[]{:S(2)}) collective-permute-start(bf16[4,160,128]{2,1,0:T(8,128)(2,1)S(1)} %bitcast.136), channel_id=1, source_target_pairs={{6,0},{12,6},{18,12},{24,18},{30,24},{36,30},{42,36},{48,42},{54,4... | collective-permute-start | bytes 491528 | tf_op jit(solution)/shard_map/ppermute | solution.py:22
  54.6 1.9 collective-permute-start
  56.6 0.0 copy-done.1
  56.6 0.1 copy.21
  56.7 0.1 reshape.56
  56.8 0.6 copy.28
  57.4 2.4 %collective-permute-done.1 = bf16[4,160,128]{2,1,0:T(8,128)(2,1)S(1)} collective-permute-done((bf16[4,160,128]{2,1,0:T(8,128)(2,1)S(1)}, bf16[4,160,128]{2,1,0:T(8,128)(2,1)S(1)}, u32[]{:S(2)}, u32[]{:S(2)}) %collective-permute-start.1) | collective-permute-done | bytes 163872 | tf_op jit(solution)/shard_map/ppermute | solution.py:22
  59.8 12.1 %collective-permute-done = bf16[4,160,128]{2,1,0:T(8,128)(2,1)S(1)} collective-permute-done((bf16[4,160,128]{2,1,0:T(8,128)(2,1)S(1)}, bf16[4,160,128]{2,1,0:T(8,128)(2,1)S(1)}, u32[]{:S(2)}, u32[]{:S(2)}) %collective-permute-start) | collective-permute-done | bytes 163872 | tf_op jit(solution)/shard_map/ppermute | solution.py:19
  71.9 0.1 pad_maximum_fusion
  72.0 2.4 %gather_fusion = bf16[60,160,128]{2,1,0:T(8,128)(2,1)} fusion(bf16[20,160,128]{2,1,0:T(8,128)(2,1)S(1)} %pad_maximum_fusion, s32[1024]{0:T(1024)S(1)} %pad_clamp_fusion), kind=kCustom, calls=%fused_computation | custom fusion | bytes 4915440 | tf_op jit(solution)/shard_map/gather | solution.py:59
  74.4 4.3 %fusion.22 = bf16[12,160,128]{2,1,0:T(8,128)(2,1)S(1)} fusion(bf16[12,5,160,160]{3,2,1,0:T(8,128)(2,1)} %param.9, bf16[12,5,160,128]{3,2,1,0:T(8,128)(2,1)} %bitcast.129, bf16[12,160,128]{2,1,0:T(8,128)(2,1)S(1)} %bitcast.131, f32[12,160]{1,0:T(8,128)S(1)} %fusion.25), kind=kOutput, calls=%fused_computation.31 | convolution fusion | flops 394690560 | bytes 6520320 | tf_op jit(solution)/shard_map/ekij,ekjs->eis/dot_general | solution.py:32
  78.7 1.9 collective-permute-start.2
  80.7 14.2 %collective-permute-start.3 = (bf16[4,160,128]{2,1,0:T(8,128)(2,1)S(1)}, bf16[4,160,128]{2,1,0:T(8,128)(2,1)S(1)}, u32[]{:S(2)}, u32[]{:S(2)}) collective-permute-start(bf16[4,160,128]{2,1,0:T(8,128)(2,1)S(1)} %get-tuple-element.12), channel_id=1, source_target_pairs={{6,0},{12,6},{18,12},{24,18},{30,24},{36,30},{42,36},{48,42},{54,4... | collective-permute-start | bytes 491528 | tf_op jit(solution)/shard_map/ppermute | solution.py:22
  94.8 7.0 %collective-permute-done.2 = bf16[4,160,128]{2,1,0:T(8,128)(2,1)S(1)} collective-permute-done((bf16[4,160,128]{2,1,0:T(8,128)(2,1)S(1)}, bf16[4,160,128]{2,1,0:T(8,128)(2,1)S(1)}, u32[]{:S(2)}, u32[]{:S(2)}) %collective-permute-start.2) | collective-permute-done | bytes 163872 | tf_op jit(solution)/shard_map/ppermute | solution.py:19
  101.9 0.0 collective-permute-done.3
  101.9 0.1 pad_maximum_fusion.1
  102.0 2.4 %gather_fusion.1 = bf16[60,160,128]{2,1,0:T(8,128)(2,1)} fusion(bf16[20,160,128]{2,1,0:T(8,128)(2,1)S(1)} %pad_maximum_fusion.1, s32[1024]{0:T(1024)S(1)} %pad_clamp_fusion), kind=kCustom, calls=%fused_computation.1 | custom fusion | bytes 4915440 | tf_op jit(solution)/shard_map/gather | solution.py:59
  104.3 4.4 %fusion.21 = bf16[12,160,128]{2,1,0:T(8,128)(2,1)S(1)} fusion(bf16[12,5,160,160]{3,2,1,0:T(8,128)(2,1)} %param.9, bf16[12,5,160,128]{3,2,1,0:T(8,128)(2,1)} %bitcast.127, bf16[12,160,128]{2,1,0:T(8,128)(2,1)S(1)} %bitcast.132, bf16[12,160,128]{2,1,0:T(8,128)(2,1)S(1)} %fusion.22, f32[12,160]{1,0:T(8,128)S(1)} %fusion.25), kind=kOutput, calls=%fused_computation.30 | convolution fusion | flops 395182080 | bytes 7011840 | tf_op jit(solution)/shard_map/ekij,ekjs->eis/dot_general | solution.py:32
  108.7 1.9 collective-permute-start.4
  110.7 14.2 %collective-permute-start.5 = (bf16[4,160,128]{2,1,0:T(8,128)(2,1)S(1)}, bf16[4,160,128]{2,1,0:T(8,128)(2,1)S(1)}, u32[]{:S(2)}, u32[]{:S(2)}) collective-permute-start(bf16[4,160,128]{2,1,0:T(8,128)(2,1)S(1)} %get-tuple-element.10), channel_id=1, source_target_pairs={{6,0},{12,6},{18,12},{24,18},{30,24},{36,30},{42,36},{48,42},{54,4... | collective-permute-start | bytes 491528 | tf_op jit(solution)/shard_map/ppermute | solution.py:22
  124.9 1.5 collective-permute-done.4
  126.3 9.7 %collective-permute-done.5 = bf16[4,160,128]{2,1,0:T(8,128)(2,1)S(1)} collective-permute-done((bf16[4,160,128]{2,1,0:T(8,128)(2,1)S(1)}, bf16[4,160,128]{2,1,0:T(8,128)(2,1)S(1)}, u32[]{:S(2)}, u32[]{:S(2)}) %collective-permute-start.5) | collective-permute-done | bytes 163872 | tf_op jit(solution)/shard_map/ppermute | solution.py:22
  136.1 0.1 pad_maximum_fusion.2
  136.2 2.4 %gather_fusion.2 = bf16[60,160,128]{2,1,0:T(8,128)(2,1)} fusion(bf16[20,160,128]{2,1,0:T(8,128)(2,1)S(1)} %pad_maximum_fusion.2, s32[1024]{0:T(1024)S(1)} %pad_clamp_fusion), kind=kCustom, calls=%fused_computation.2 | custom fusion | bytes 4915440 | tf_op jit(solution)/shard_map/gather | solution.py:59
  138.5 4.4 %fusion.20 = bf16[12,160,128]{2,1,0:T(8,128)(2,1)S(1)} fusion(bf16[12,5,160,160]{3,2,1,0:T(8,128)(2,1)} %param.9, bf16[12,5,160,128]{3,2,1,0:T(8,128)(2,1)} %bitcast.128, bf16[12,160,128]{2,1,0:T(8,128)(2,1)S(1)} %fusion.22, bf16[12,160,128]{2,1,0:T(8,128)(2,1)S(1)} %fusion.21, f32[12,160]{1,0:T(8,128)S(1)} %fusion.25), kind=kOutput, calls=%fused_computation.29 | convolution fusion | flops 395182080 | bytes 7011840 | tf_op jit(solution)/shard_map/ekij,ekjs->eis/dot_general | solution.py:32
  142.9 1.9 collective-permute-start.6
  144.9 14.4 %collective-permute-start.7 = (bf16[4,160,128]{2,1,0:T(8,128)(2,1)S(1)}, bf16[4,160,128]{2,1,0:T(8,128)(2,1)S(1)}, u32[]{:S(2)}, u32[]{:S(2)}) collective-permute-start(bf16[4,160,128]{2,1,0:T(8,128)(2,1)S(1)} %get-tuple-element.8), channel_id=1, source_target_pairs={{6,0},{12,6},{18,12},{24,18},{30,24},{36,30},{42,36},{48,42},{54,4... | collective-permute-start | bytes 491528 | tf_op jit(solution)/shard_map/ppermute | solution.py:22
  159.3 7.6 %collective-permute-done.6 = bf16[4,160,128]{2,1,0:T(8,128)(2,1)S(1)} collective-permute-done((bf16[4,160,128]{2,1,0:T(8,128)(2,1)S(1)}, bf16[4,160,128]{2,1,0:T(8,128)(2,1)S(1)}, u32[]{:S(2)}, u32[]{:S(2)}) %collective-permute-start.6) | collective-permute-done | bytes 163872 | tf_op jit(solution)/shard_map/ppermute | solution.py:19
  166.9 0.0 collective-permute-done.7
  166.9 0.1 pad_maximum_fusion.3
  167.0 2.4 %gather_fusion.3 = bf16[60,160,128]{2,1,0:T(8,128)(2,1)} fusion(bf16[20,160,128]{2,1,0:T(8,128)(2,1)S(1)} %pad_maximum_fusion.3, s32[1024]{0:T(1024)S(1)} %pad_clamp_fusion), kind=kCustom, calls=%fused_computation.3 | custom fusion | bytes 4915440 | tf_op jit(solution)/shard_map/gather | solution.py:59
  169.4 4.4 %fusion.19 = bf16[12,160,128]{2,1,0:T(8,128)(2,1)S(1)} fusion(bf16[12,5,160,160]{3,2,1,0:T(8,128)(2,1)} %param.9, bf16[12,5,160,128]{3,2,1,0:T(8,128)(2,1)} %bitcast.126, bf16[12,160,128]{2,1,0:T(8,128)(2,1)S(1)} %fusion.21, bf16[12,160,128]{2,1,0:T(8,128)(2,1)S(1)} %fusion.20, f32[12,160]{1,0:T(8,128)S(1)} %fusion.25), kind=kOutput, calls=%fused_computation.28 | convolution fusion | flops 395182080 | bytes 7011840 | tf_op jit(solution)/shard_map/ekij,ekjs->eis/dot_general | solution.py:32
  173.8 21.1 %all_to_all.36 = bf16[12,160,128]{2,1,0:T(8,128)(2,1)S(1)} all-to-all(bf16[12,160,128]{2,1,0:T(8,128)(2,1)S(1)} %fusion.19), channel_id=1, replica_groups=mesh['elem'=128,'state'=6] {'state'}, dimensions={0} | all-to-all | bytes 983040 | tf_op jit(solution)/shard_map/all_to_all | solution.py:76
  194.9 0.3 copy.30
  195.2 1.4 all_to_all.33
  (8 shorter events, 0.1 us)
Async XLA Ops:
  0.0 1.3 copy-start
  1.3 15.7 %copy-start.2 = (s32[12]{0:T(128)S(1)}, s32[12]{0:T(128)}, u32[]{:S(2)}) copy-start(s32[12]{0:T(128)} %param.7) | copy-start | bytes 148
  4.7 51.9 %copy-start.1 = (s32[12,5]{0,1:T(8,128)S(1)}, s32[12,5]{0,1:T(8,128)}, u32[]{:S(2)}) copy-start(s32[12,5]{0,1:T(8,128)} %param.8) | copy-start | bytes 724
  4.7 34.6 %all-to-all-start = ((bf16[2,160,768]{1,0,2:T(2,128)(2,1)}), bf16[2,160,768]{1,0,2:T(2,128)(2,1)S(1)}, u32[]{:S(2)}, u32[]{:S(2)}) async-start(bf16[2,160,768]{1,0,2:T(2,128)(2,1)} %copy.16), calls=%async_computation | async-start | bytes 1572864 | tf_op jit(solution)/shard_map/all_to_all | solution.py:49
  40.9 18.9 %collective-permute-start.1 = (bf16[4,160,128]{2,1,0:T(8,128)(2,1)S(1)}, bf16[4,160,128]{2,1,0:T(8,128)(2,1)S(1)}, u32[]{:S(2)}, u32[]{:S(2)}) collective-permute-start(bf16[4,160,128]{2,1,0:T(8,128)(2,1)S(1)} %bitcast.136), channel_id=1, source_target_pairs={{6,0},{12,6},{18,12},{24,18},{30,24},{36,30},{42,36},{48,42},{54,4... | collective-permute-start | bytes 491528 | tf_op jit(solution)/shard_map/ppermute | solution.py:22
  54.6 17.3 %collective-permute-start = (bf16[4,160,128]{2,1,0:T(8,128)(2,1)S(1)}, bf16[4,160,128]{2,1,0:T(8,128)(2,1)S(1)}, u32[]{:S(2)}, u32[]{:S(2)}) collective-permute-start(bf16[4,160,128]{2,1,0:T(8,128)(2,1)S(1)} %bitcast.135), channel_id=1, source_target_pairs={{0,6},{6,12},{12,18},{18,24},{24,30},{30,36},{36,42},{42,48},{48,5... | collective-permute-start | bytes 491528 | tf_op jit(solution)/shard_map/ppermute | solution.py:19
  78.7 23.1 %collective-permute-start.2 = (bf16[4,160,128]{2,1,0:T(8,128)(2,1)S(1)}, bf16[4,160,128]{2,1,0:T(8,128)(2,1)S(1)}, u32[]{:S(2)}, u32[]{:S(2)}) collective-permute-start(bf16[4,160,128]{2,1,0:T(8,128)(2,1)S(1)} %get-tuple-element.11), channel_id=1, source_target_pairs={{0,6},{6,12},{12,18},{18,24},{24,30},{30,36},{36,42},{42,48},{48,5... | collective-permute-start | bytes 491528 | tf_op jit(solution)/shard_map/ppermute | solution.py:19
  80.7 21.2 %collective-permute-start.3 = (bf16[4,160,128]{2,1,0:T(8,128)(2,1)S(1)}, bf16[4,160,128]{2,1,0:T(8,128)(2,1)S(1)}, u32[]{:S(2)}, u32[]{:S(2)}) collective-permute-start(bf16[4,160,128]{2,1,0:T(8,128)(2,1)S(1)} %get-tuple-element.12), channel_id=1, source_target_pairs={{6,0},{12,6},{18,12},{24,18},{30,24},{36,30},{42,36},{48,42},{54,4... | collective-permute-start | bytes 491528 | tf_op jit(solution)/shard_map/ppermute | solution.py:22
  108.7 17.6 %collective-permute-start.4 = (bf16[4,160,128]{2,1,0:T(8,128)(2,1)S(1)}, bf16[4,160,128]{2,1,0:T(8,128)(2,1)S(1)}, u32[]{:S(2)}, u32[]{:S(2)}) collective-permute-start(bf16[4,160,128]{2,1,0:T(8,128)(2,1)S(1)} %get-tuple-element.9), channel_id=1, source_target_pairs={{0,6},{6,12},{12,18},{18,24},{24,30},{30,36},{36,42},{42,48},{48,5... | collective-permute-start | bytes 491528 | tf_op jit(solution)/shard_map/ppermute | solution.py:19
  110.7 25.4 %collective-permute-start.5 = (bf16[4,160,128]{2,1,0:T(8,128)(2,1)S(1)}, bf16[4,160,128]{2,1,0:T(8,128)(2,1)S(1)}, u32[]{:S(2)}, u32[]{:S(2)}) collective-permute-start(bf16[4,160,128]{2,1,0:T(8,128)(2,1)S(1)} %get-tuple-element.10), channel_id=1, source_target_pairs={{6,0},{12,6},{18,12},{24,18},{30,24},{36,30},{42,36},{48,42},{54,4... | collective-permute-start | bytes 491528 | tf_op jit(solution)/shard_map/ppermute | solution.py:22
  142.9 24.0 %collective-permute-start.6 = (bf16[4,160,128]{2,1,0:T(8,128)(2,1)S(1)}, bf16[4,160,128]{2,1,0:T(8,128)(2,1)S(1)}, u32[]{:S(2)}, u32[]{:S(2)}) collective-permute-start(bf16[4,160,128]{2,1,0:T(8,128)(2,1)S(1)} %get-tuple-element.7), channel_id=1, source_target_pairs={{0,6},{6,12},{12,18},{18,24},{24,30},{30,36},{36,42},{42,48},{48,5... | collective-permute-start | bytes 491528 | tf_op jit(solution)/shard_map/ppermute | solution.py:19
  144.9 22.1 %collective-permute-start.7 = (bf16[4,160,128]{2,1,0:T(8,128)(2,1)S(1)}, bf16[4,160,128]{2,1,0:T(8,128)(2,1)S(1)}, u32[]{:S(2)}, u32[]{:S(2)}) collective-permute-start(bf16[4,160,128]{2,1,0:T(8,128)(2,1)S(1)} %get-tuple-element.8), channel_id=1, source_target_pairs={{6,0},{12,6},{18,12},{24,18},{30,24},{36,30},{42,36},{48,42},{54,4... | collective-permute-start | bytes 491528 | tf_op jit(solution)/shard_map/ppermute | solution.py:22
where the time goes:
time: 197 us
  starting transfers between devices  76.4 us (39%)
  waiting for transfers between devices  62.6 us (32%)
  blocking collectives  21.1 us (11%)
  matrix products  19.1 us (10%)
  local copies, waits for them, and re-layouts  16.6 us (8%)
    ppermute x4, starting transfers between devices, with_halo(): lax.ppermute(lax.slice_in_dim(block, 0, width, axis=dim), axis, backward)  56.5 us
    ppermute x4, waiting for transfers between devices, with_halo(): lax.ppermute(lax.slice_in_dim(block, block.shape[dim] - width, None, axis...  28.2 us
    all_to_all x1, waiting for transfers between devices, on_device(): lax.all_to_all(start_rows, 'state', split_axis=2, concat_axis=0, tiled=True)  22.2 us
    all_to_all x1, blocking collectives, on_device(): lax.all_to_all(current, 'state', split_axis=0, concat_axis=2, tiled=True)  21.1 us
    dot_general x4, matrix products, coupled(): jnp.einsum('ekij,ekjs->eis', block_part, gathered, preferred_element_type...  17.5 us
    all_to_all x1, starting transfers between devices, on_device(): lax.all_to_all(start_rows, 'state', split_axis=2, concat_axis=0, tiled=True)  12.3 us
    ppermute x4, waiting for transfers between devices, with_halo(): lax.ppermute(lax.slice_in_dim(block, 0, width, axis=dim), axis, backward)  12.1 us
    gather x4, local copies, waits for them, and re-layouts, image_of(): image = coupled(blocks, padded[local_source])  9.42 us
  transfers between devices with their start and end apart: 9, of which 7 were waited for; matrix products, arithmetic and copies ran while one was open for 0% of the time, Pallas kernels for 0%

commit v1 on v0

v1 whole, which is shorter than its diff:
```python
import functools

import jax
import jax.numpy as jnp
from jax import lax
from jax.experimental import pallas as pl
from jax.experimental.pallas import tpu as pltpu
from jax.sharding import PartitionSpec as P

MESH = pl.DeviceIdType.MESH
DEG = 4
center_shift = 0.2
half_span = 1.1


def kernel(
    n_elem, n_state, counts, neighbors, orbitals, rotation, blocks_hbm, out,
    fields, far_halo, near_halo, last, staged, blocks, blocks_sem,
    a2a_send, a2a_recv, far_send, far_recv, near_send, near_recv, out_send, out_recv, own_sem,
):
    me, spot = lax.axis_index("elem"), lax.axis_index("state")
    core = lax.rem(me, 2)
    high = lax.rem(me // 2, 2)
    elems, reach = last.shape[0], 4
    half = reach // 2
    rows, width = fields.shape[2], fields.shape[3]
    total = n_elem * elems

    def block_at(place):
        return jnp.where(high == 0, place, n_state - 1 - place)

    mine = block_at(spot)
    far = lax.rem(me + jnp.where(core == 0, n_elem - 1, 1), n_elem)
    far_id = (far, n_state - 1 - spot)
    near_id = (me + 1 - 2 * core, spot)

    load = pltpu.make_async_copy(blocks_hbm, blocks, blocks_sem)
    load.start()

    barrier = pltpu.get_barrier_semaphore()
    for step in range(1, n_state):
        pl.semaphore_signal(
            barrier, inc=1, device_id=(me, lax.rem(spot + step, n_state)), device_id_type=MESH
        )
    for device in (far_id, near_id):
        pl.semaphore_signal(barrier, inc=1, device_id=device, device_id_type=MESH)

    row = lax.broadcasted_iota(jnp.int32, (rows, width), 0)
    limits = [counts[2 * spot], counts[2 * spot + 1]]

    def rotated(place):
        columns = pl.ds(pl.multiple_of(block_at(place) * width, width), width)
        result = jnp.dot(
            orbitals[...], rotation[:, columns], preferred_element_type=jnp.float32
        )
        return [
            jnp.where(row < limits[a], result[a * rows:(a + 1) * rows], 0.0).astype(jnp.bfloat16)
            for a in range(2)
        ]

    def a2a_copy(step):
        place = lax.rem(spot + step, n_state)
        return pltpu.make_async_remote_copy(
            src_ref=staged.at[step],
            dst_ref=fields.at[0, pl.ds(reach + 2 * spot, 2)],
            send_sem=a2a_send.at[step],
            recv_sem=a2a_recv.at[spot],
            device_id=(me, place),
            device_id_type=MESH,
        )

    def stage(step):
        pair = rotated(lax.rem(spot + step, n_state))
        for a in range(2):
            staged[step, a] = pair[a]

    stage(1)
    pl.semaphore_wait(barrier, n_state + 1)
    a2a_copy(1).start()

    @pl.loop(2, n_state)
    def _(step):
        stage(step)
        a2a_copy(step).start()

    own = rotated(spot)
    for a in range(2):
        fields[0, reach + 2 * spot + a] = own[a]

    def arrived(pair):
        @pl.when(pair != spot)
        def _():
            pltpu.make_async_remote_copy(
                src_ref=staged.at[0],
                dst_ref=fields.at[0, pl.ds(reach + 2 * pair, 2)],
                send_sem=a2a_send.at[0],
                recv_sem=a2a_recv.at[pair],
                device_id=(me, pair),
                device_id_type=MESH,
            ).wait_recv()

    far_own = jnp.where(core == 0, 0, elems - reach)
    near_own = jnp.where(core == 0, elems - reach, 0)
    far_slot = jnp.where(core == 0, 0, elems + reach)
    near_slot = jnp.where(core == 0, elems + reach, 0)

    def halo(level, side, piece):
        first, landing, device, send, recv = (
            (far_own, far_halo, far_id, far_send, far_recv)
            if side == "far"
            else (near_own, near_halo, near_id, near_send, near_recv)
        )
        return pltpu.make_async_remote_copy(
            src_ref=fields.at[level, pl.ds(reach + first + 2 * piece, 2)],
            dst_ref=landing.at[level, pl.ds(2 * piece, 2)],
            send_sem=send.at[level, piece],
            recv_sem=recv.at[level, piece],
            device_id=device,
            device_id_type=MESH,
        )

    for side, first in (("far", far_own), ("near", near_own)):
        for piece in range(half):
            arrived(first // 2 + piece)
            halo(0, side, piece).start()
    for pair in range(half, elems // 2 - half):
        arrived(pair)
    load.wait()

    start_of_all = me * elems - reach

    def updated(level, e):
        image = jnp.zeros((rows, width), jnp.float32)
        for k in range(5):
            source = neighbors[e, k] - start_of_all
            source = jnp.where(source < 0, source + total, source)
            source = jnp.where(source >= total, source - total, source)
            source = jnp.clip(source, 0, elems + 2 * reach - 1)
            image += jnp.dot(
                blocks[e, k], fields[level - 1, source], preferred_element_type=jnp.float32
            )
        image = jnp.where(row < counts[e], image, 0.0)
        current = fields[level - 1, reach + e].astype(jnp.float32)
        factor = (1.0 if level == 1 else 2.0) / half_span
        value = factor * (image - center_shift * current)
        if level > 1:
            value = value - fields[level - 2, reach + e].astype(jnp.float32)
        return value.astype(jnp.bfloat16)

    def pair_of(level, pair):
        @pl.loop(0, 2)
        def _(a):
            e = 2 * pair + a
            if level < DEG:
                fields[level, reach + e] = updated(level, e)
            else:
                last[e] = updated(level, e)

    def out_copy(pair, source_pair):
        columns = pl.ds(pl.multiple_of(mine * width, width), width)
        return pltpu.make_async_remote_copy(
            src_ref=last.at[pl.ds(2 * pair, 2)],
            dst_ref=out.at[:, :, columns],
            send_sem=out_send.at[pair],
            recv_sem=out_recv.at[source_pair],
            device_id=(me, pair),
            device_id_type=MESH,
        )

    columns_mine = pl.ds(pl.multiple_of(mine * width, width), width)

    def own_copy():
        return pltpu.make_async_copy(
            last.at[pl.ds(2 * spot, 2)], out.at[:, :, columns_mine], own_sem
        )

    def ship(pair):
        @pl.when(pair != spot)
        def _():
            out_copy(pair, spot).start()

        @pl.when(pair == spot)
        def _():
            own_copy().start()

    for level in range(1, DEG + 1):
        for pair in range(half, elems // 2 - half):
            pair_of(level, pair)
            if level == DEG:
                ship(pair)
        for side, first, slot, landing in (
            ("near", near_own, near_slot, near_halo), ("far", far_own, far_slot, far_halo)
        ):
            for piece in range(half):
                halo(level - 1, side, piece).wait_recv()
            fields[level - 1, pl.ds(slot, reach)] = landing[level - 1]
            for piece in range(half):
                pair = first // 2 + piece
                pair_of(level, pair)
                if level < DEG:
                    halo(level, side, piece).start()
                else:
                    ship(pair)

    for place in range(n_state):
        @pl.when(place != spot)
        def _():
            columns = pl.ds(pl.multiple_of(block_at(place) * width, width), width)
            pltpu.make_async_remote_copy(
                src_ref=last.at[pl.ds(0, 2)],
                dst_ref=out.at[:, :, columns],
                send_sem=out_send.at[place],
                recv_sem=out_recv.at[place],
                device_id=(me, place),
                device_id_type=MESH,
            ).wait_recv()
            out_copy(place, spot).wait_send()
    own_copy().wait()
    for step in range(1, n_state):
        a2a_copy(step).wait_send()
    for level in range(DEG):
        for side in ("far", "near"):
            for piece in range(half):
                halo(level, side, piece).wait_send()


def on_device(n_elem, n_state, orbitals, rotation, counts, neighbors, blocks):
    pair, rows, states = orbitals.shape
    elems = counts.shape[0]
    width = states // n_state
    vmem, smem = (pl.BlockSpec(memory_space=s) for s in (pltpu.VMEM, pltpu.SMEM))
    dma = pltpu.SemaphoreType.DMA
    return pl.pallas_call(
        functools.partial(kernel, n_elem, n_state),
        out_shape=jax.ShapeDtypeStruct((pair, rows, states), jnp.bfloat16),
        in_specs=[smem, smem, vmem, vmem, pl.BlockSpec(memory_space=pl.ANY)],
        out_specs=vmem,
        scratch_shapes=[
            pltpu.VMEM((DEG, elems + 8, rows, width), jnp.bfloat16),
            pltpu.VMEM((DEG, 4, rows, width), jnp.bfloat16),
            pltpu.VMEM((DEG, 4, rows, width), jnp.bfloat16),
            pltpu.VMEM((elems, rows, width), jnp.bfloat16),
            pltpu.VMEM((n_state, pair, rows, width), jnp.bfloat16),
            pltpu.VMEM(blocks.shape, jnp.bfloat16),
            dma,
            dma((n_state,)),
            dma((n_state,)),
            dma((DEG, 2)),
            dma((DEG, 2)),
            dma((DEG, 2)),
            dma((DEG, 2)),
            dma((n_state,)),
            dma((n_state,)),
            dma,
        ],
        compiler_params=pltpu.CompilerParams(
            collective_id=0, has_side_effects=True, vmem_limit_bytes=48 * 1024 * 1024
        ),
    )(counts, neighbors, orbitals.reshape(pair * rows, states), rotation, blocks)


def solution(mesh):
    n_elem, n_state = mesh.shape["elem"], mesh.shape["state"]
    in_specs = (
        P(("elem", "state"), None, None),
        P(),
        P("elem"),
        P("elem", None),
        P("elem", None, None, None),
    )
    return jax.shard_map(
        functools.partial(on_device, n_elem, n_state),
        mesh=mesh,
        in_specs=in_specs,
        out_specs=P(("elem", "state"), None, None),
        check_vma=False,
    )
```

time: 197 us -> 89.4 us (0.45)
  Pallas kernels: 0 us -> 84.6 us
  starting transfers between devices: 76.4 us -> 0 us
  waiting for transfers between devices: 62.6 us -> 0 us
  blocking collectives: 21.1 us -> 0 us
  matrix products: 19.1 us -> 0 us
  local copies, waits for them, and re-layouts: 16.6 us -> 4.51 us
    pallas_call x0 -> x1, Pallas kernels: none -> 84.6 us  [on_device(): pl.pallas_call(functools.partial(kernel, n_elem, n_state), out_shape=jax....]
    ppermute x8 -> x0, starting transfers between devices: 64.2 us -> none  [the longest x4 56.5 us: with_halo(): lax.ppermute(lax.slice_in_dim(block, 0, width, axis=dim), axis, backward)]
    ppermute x8 -> x0, waiting for transfers between devices: 40.3 us -> none  [the longest x4 28.2 us: with_halo(): lax.ppermute(lax.slice_in_dim(block, block.shape[dim] - width, None, axis...]
    all_to_all x1 -> x0, waiting for transfers between devices: 22.2 us -> none  [on_device(): lax.all_to_all(start_rows, 'state', split_axis=2, concat_axis=0, tiled=True)]
    all_to_all x1 -> x0, blocking collectives: 21.1 us -> none  [on_device(): lax.all_to_all(current, 'state', split_axis=0, concat_axis=2, tiled=True)]
    dot_general x5 -> x0, matrix products: 19.1 us -> none  [the longest x4 17.5 us: coupled(): jnp.einsum('ekij,ekjs->eis', block_part, gathered, preferred_element_type...]
    all_to_all x1 -> x0, starting transfers between devices: 12.3 us -> none  [on_device(): lax.all_to_all(start_rows, 'state', split_axis=2, concat_axis=0, tiled=True)]
    gather x4 -> x0, local copies, waits for them, and re-layouts: 9.42 us -> none  [image_of(): image = coupled(blocks, padded[local_source])]
  transfers between devices with their start and end apart: 9 -> 0, of which waited for: 7 -> 0; matrix products, arithmetic and copies ran while one was open for 0% -> 0% of each run, Pallas kernels for 0% -> 0%
where the time goes in v1:
time: 89.4 us; the launch traced here: 89.2 us
  Pallas kernels  84.6 us (95%)
  local copies, waits for them, and re-layouts  4.51 us (5%)
    pallas_call x1, Pallas kernels, on_device(): pl.pallas_call(functools.partial(kernel, n_elem, n_state), out_shape=jax....  84.6 us
    unnamed x8, local copies, waits for them, and re-layouts  4.51 us

profile of v1, /device:TPU:64, one launch (start us, length us, event | category | flops | bytes accessed | tf_op | source)
XLA Modules:
  0.0 89.2 jit_solution(6747449172748894895)
XLA Ops:
  0.0 0.8 copy.6.neighbors
  0.8 0.0 copy-start
  0.8 1.3 %copy-done = bf16[768,768]{1,0:T(8,128)(2,1)S(1)} copy-done((bf16[768,768]{1,0:T(8,128)(2,1)S(1)}, bf16[768,768]{1,0:T(8,128)(2,1)}, u32[]{:S(2)}) %copy-start) | copy-done | bytes 1179672
  2.0 0.0 copy-start.1
  2.0 1.0 %copy-done.1 = bf16[2,160,768]{2,1,0:T(8,128)(2,1)S(1)} copy-done((bf16[2,160,768]{2,1,0:T(8,128)(2,1)S(1)}, bf16[2,160,768]{2,1,0:T(8,128)(2,1)}, u32[]{:S(2)}) %copy-start.1) | copy-done | bytes 491544
  3.1 0.0 copy-start.2
  3.1 0.7 copy-done.2
  3.7 84.6 %shard_map.55 = bf16[2,160,768]{2,1,0:T(8,128)(2,1)S(1)} custom-call(s32[12]{0:T(128)S(1)} %copy-done.2, s32[12,5]{1,0:T(8,128)S(1)} %copy.6.neighbors, bf16[320,768]{1,0:T(8,128)(2,1)S(1)} %bitcast.1, bf16[768,768]{1,0:T(8,128)(2,1)S(1)} %copy-done, bf16[12,5,160,160]{3,2,1,0:T(8,128)(2,1)} %blocks_hbm.1), custom_call_target="tpu_custom_call" | custom-call | tf_op jit(solution)/shard_map/pallas_call | solution.py:233
  88.4 0.8 copy.8
Async XLA Ops:
  0.8 1.3 %copy-start = (bf16[768,768]{1,0:T(8,128)(2,1)S(1)}, bf16[768,768]{1,0:T(8,128)(2,1)}, u32[]{:S(2)}) copy-start(bf16[768,768]{1,0:T(8,128)(2,1)} %rotation.1) | copy-start | bytes 3538948
  2.0 1.0 %copy-start.1 = (bf16[2,160,768]{2,1,0:T(8,128)(2,1)S(1)}, bf16[2,160,768]{2,1,0:T(8,128)(2,1)}, u32[]{:S(2)}) copy-start(bf16[2,160,768]{2,1,0:T(8,128)(2,1)} %param.5) | copy-start | bytes 1474564
  3.1 0.7 copy-start.2

commit v2 on v1

v2 whole, which is shorter than its diff:
```python
import functools

import jax
import jax.numpy as jnp
from jax import lax
from jax.experimental import pallas as pl
from jax.experimental.pallas import tpu as pltpu
from jax.sharding import PartitionSpec as P

MESH = pl.DeviceIdType.MESH
DEG = 4
center_shift = 0.2
half_span = 1.1


def kernel(
    n_elem, n_state, counts_hbm, neighbors_hbm, orbitals_hbm, rotation_hbm, blocks_hbm, out,
    counts, neighbors, orbitals, rotation, load_sem, fields, far_out, far_halo, near_halo, last,
    staged, landed, homed, blocks, scratch, own_counts, far_counts, count_send, count_recv,
    a2a_send, a2a_recv, far_send, far_recv, near_send, near_recv, out_send, out_recv,
):
    me, spot = lax.axis_index("elem"), lax.axis_index("state")
    core = lax.rem(me, 2)
    high = lax.rem(me // 2, 2)
    elems, reach = counts.shape[0], 4
    half = reach // 2
    rows, width = fields.shape[2], fields.shape[3]
    total = n_elem * elems

    def block_at(place):
        return jnp.where(high == 0, place, n_state - 1 - place)

    mine = block_at(spot)
    far = lax.rem(me + jnp.where(core == 0, n_elem - 1, 1), n_elem)
    far_id = (far, n_state - 1 - spot)
    near_id = (me + 1 - 2 * core, spot)

    loads = [
        pltpu.make_async_copy(source, target, load_sem.at[i])
        for i, (source, target) in enumerate([
            (counts_hbm, counts), (orbitals_hbm, orbitals), (rotation_hbm, rotation),
            (neighbors_hbm, neighbors), (blocks_hbm, blocks),
        ])
    ]
    for load in loads:
        load.start()

    barrier = pltpu.get_barrier_semaphore()
    for step in range(1, n_state):
        pl.semaphore_signal(
            barrier, inc=1, device_id=(me, lax.rem(spot + step, n_state)), device_id_type=MESH
        )
    for device in (far_id, near_id):
        pl.semaphore_signal(barrier, inc=1, device_id=device, device_id_type=MESH)

    for load in loads[:3]:
        load.wait()
    row = lax.broadcasted_iota(jnp.int32, (rows, width), 0)
    main = 128
    tail = rows - main
    tail_row = row[:tail]
    flip = (
        lax.broadcasted_iota(jnp.int32, (tail, tail), 0)
        + lax.broadcasted_iota(jnp.int32, (tail, tail), 1)
        == tail - 1
    ).astype(jnp.bfloat16)

    def flipped(part):
        return jnp.dot(flip, part, preferred_element_type=jnp.float32).astype(jnp.bfloat16)

    def pack(target, first, second):
        target[0:main] = first[:main]
        target[main:2 * main] = second[:main]
        target[2 * main:] = first[main:] + flipped(second[main:])

    def unpack(source, limit_first, limit_second):
        shared = source[2 * main:]
        zero = jnp.zeros_like(shared)
        return (
            jnp.where(tail_row < limit_first - main, shared, zero),
            jnp.where(tail_row < limit_second - main, flipped(shared), zero),
        )

    def a2a_copy(place):
        return pltpu.make_async_remote_copy(
            src_ref=staged.at[place],
            dst_ref=landed.at[spot],
            send_sem=a2a_send.at[place],
            recv_sem=a2a_recv.at[spot],
            device_id=(me, place),
            device_id_type=MESH,
        )

    def place_at(step):
        return jnp.where(lax.rem(step, 2) == 0, step // 2, n_state - 1 - step // 2)

    limits = [counts[2 * spot], counts[2 * spot + 1]]

    def stage(step):
        place = place_at(step)
        columns = pl.ds(pl.multiple_of(block_at(place) * width, width), width)
        result = jnp.dot(
            orbitals[...], rotation[:, columns], preferred_element_type=jnp.float32
        )
        first, second = [
            jnp.where(row < limits[a], result[a * rows:(a + 1) * rows], 0.0).astype(jnp.bfloat16)
            for a in range(2)
        ]
        pack(staged.at[place], first, second)

    def send(step):
        place = place_at(step)

        @pl.when(place != spot)
        def _():
            a2a_copy(place).start()

    far_own = jnp.where(core == 0, 0, elems - reach)
    for j in range(reach):
        own_counts[j] = jnp.full((8, width), counts[far_own + j], jnp.int32)
    count_copy = pltpu.make_async_remote_copy(
        src_ref=own_counts,
        dst_ref=far_counts,
        send_sem=count_send,
        recv_sem=count_recv,
        device_id=far_id,
        device_id_type=MESH,
    )
    stage(0)
    pl.semaphore_wait(barrier, n_state + 1)
    send(0)
    count_copy.start()

    @pl.loop(1, n_state)
    def _(step):
        stage(step)
        send(step)

    def arrived(pair):
        @pl.when(pair != spot)
        def _():
            pltpu.make_async_remote_copy(
                src_ref=staged.at[0],
                dst_ref=landed.at[pair],
                send_sem=a2a_send.at[0],
                recv_sem=a2a_recv.at[pair],
                device_id=(me, pair),
                device_id_type=MESH,
            ).wait_recv()

        @pl.when(pair == spot)
        def _():
            landed[pair] = staged[pair]

    def settle(pair):
        fields_pair(landed.at[pair], 0, reach + 2 * pair, counts[2 * pair], counts[2 * pair + 1])

    def fields_pair(source, level, slot, limit_first, limit_second):
        tails = unpack(source, limit_first, limit_second)
        for a in range(2):
            fields[level, slot + a, 0:main] = source[a * main:(a + 1) * main]
            fields[level, slot + a, main:] = tails[a]

    near_own = jnp.where(core == 0, elems - reach, 0)
    far_slot = jnp.where(core == 0, 0, elems + reach)
    near_slot = jnp.where(core == 0, elems + reach, 0)

    def far_copy(level, piece):
        return pltpu.make_async_remote_copy(
            src_ref=landed.at[far_own // 2 + piece] if level == 0 else far_out.at[level, piece],
            dst_ref=far_halo.at[level, piece],
            send_sem=far_send.at[level, piece],
            recv_sem=far_recv.at[level, piece],
            device_id=far_id,
            device_id_type=MESH,
        )

    def near_copy(level, piece):
        return pltpu.make_async_remote_copy(
            src_ref=fields.at[level, pl.ds(reach + near_own + 2 * piece, 2)],
            dst_ref=near_halo.at[level, pl.ds(2 * piece, 2)],
            send_sem=near_send.at[level, piece],
            recv_sem=near_recv.at[level, piece],
            device_id=near_id,
            device_id_type=MESH,
        )

    for piece in range(half):
        arrived(far_own // 2 + piece)
        far_copy(0, piece).start()
    for piece in range(half):
        pair = near_own // 2 + piece
        arrived(pair)
        settle(pair)
        near_copy(0, piece).start()
    for piece in range(half):
        settle(far_own // 2 + piece)
    for pair in range(half, elems // 2 - half):
        arrived(pair)
        settle(pair)
    count_copy.wait()
    for load in loads[3:]:
        load.wait()

    start_of_all = me * elems - reach

    def updated(level, e):
        image = jnp.zeros((rows, width), jnp.float32)
        for k in range(5):
            source = neighbors[k, e] - start_of_all
            source = jnp.where(source < 0, source + total, source)
            source = jnp.where(source >= total, source - total, source)
            source = jnp.clip(source, 0, elems + 2 * reach - 1)
            image += jnp.dot(
                blocks[e, k], fields[level - 1, source], preferred_element_type=jnp.float32
            )
        image = jnp.where(row < counts[e], image, 0.0)
        current = fields[level - 1, reach + e].astype(jnp.float32)
        factor = (1.0 if level == 1 else 2.0) / half_span
        value = factor * (image - center_shift * current)
        if level > 1:
            value = value - fields[level - 2, reach + e].astype(jnp.float32)
        return value.astype(jnp.bfloat16)

    def pair_of(level, pair):
        if level < DEG:
            @pl.loop(0, 2)
            def _(a):
                e = 2 * pair + a
                fields[level, reach + e] = updated(level, e)
        else:
            @pl.loop(0, 2)
            def _(a):
                scratch[a] = updated(level, 2 * pair + a)

            pack(last.at[pair], scratch[0], scratch[1])

    def out_copy(pair):
        return pltpu.make_async_remote_copy(
            src_ref=last.at[pair],
            dst_ref=homed.at[spot],
            send_sem=out_send.at[pair],
            recv_sem=out_recv.at[spot],
            device_id=(me, pair),
            device_id_type=MESH,
        )

    def ship(pair):
        @pl.when(pair != spot)
        def _():
            out_copy(pair).start()

    for level in range(1, DEG + 1):
        for pair in range(half, elems // 2 - half):
            pair_of(level, pair)
            if level == DEG:
                ship(pair)
        for piece in range(half):
            near_copy(level - 1, piece).wait_recv()
        fields[level - 1, pl.ds(near_slot, reach)] = near_halo[level - 1]
        for piece in range(half):
            pair = near_own // 2 + piece
            pair_of(level, pair)
            if level < DEG:
                near_copy(level, piece).start()
            else:
                ship(pair)
        for piece in range(half):
            far_copy(level - 1, piece).wait_recv()
            fields_pair(
                far_halo.at[level - 1, piece],
                level - 1,
                far_slot + 2 * piece,
                far_counts[2 * piece, 0:1],
                far_counts[2 * piece + 1, 0:1],
            )
        for piece in range(half):
            pair = far_own // 2 + piece
            pair_of(level, pair)
            if level < DEG:
                slot = reach + 2 * pair
                pack(far_out.at[level, piece], fields[level, slot], fields[level, slot + 1])
                far_copy(level, piece).start()
            else:
                ship(pair)

    def deliver(source, place):
        columns = pl.ds(pl.multiple_of(block_at(place) * width, width), width)
        tails = unpack(source, limits[0], limits[1])
        for a in range(2):
            out[a, 0:main, columns] = source[a * main:(a + 1) * main]
            out[a, main:, columns] = tails[a]

    deliver(last.at[spot], spot)
    for step in range(1, n_state):
        place = lax.rem(spot + step, n_state)
        pltpu.make_async_remote_copy(
            src_ref=last.at[0],
            dst_ref=homed.at[place],
            send_sem=out_send.at[place],
            recv_sem=out_recv.at[place],
            device_id=(me, place),
            device_id_type=MESH,
        ).wait_recv()
        deliver(homed.at[place], place)
        out_copy(place).wait_send()
        a2a_copy(place).wait_send()
    for level in range(DEG):
        for piece in range(half):
            far_copy(level, piece).wait_send()
            near_copy(level, piece).wait_send()


def on_device(n_elem, n_state, orbitals, rotation, counts, neighbors, blocks):
    pair, rows, states = orbitals.shape
    elems = counts.shape[0]
    width = states // n_state
    packed = 2 * rows - 32
    dma = pltpu.SemaphoreType.DMA
    return pl.pallas_call(
        functools.partial(kernel, n_elem, n_state),
        out_shape=jax.ShapeDtypeStruct((pair, rows, states), jnp.bfloat16),
        in_specs=[pl.BlockSpec(memory_space=pltpu.HBM)] * 5,
        out_specs=pl.BlockSpec(memory_space=pltpu.VMEM),
        scratch_shapes=[
            pltpu.SMEM(counts.shape, jnp.int32),
            pltpu.SMEM(neighbors.shape[::-1], jnp.int32),
            pltpu.VMEM((pair * rows, states), jnp.bfloat16),
            pltpu.VMEM(rotation.shape, jnp.bfloat16),
            dma((5,)),
            pltpu.VMEM((DEG, elems + 8, rows, width), jnp.bfloat16),
            pltpu.VMEM((DEG, 2, packed, width), jnp.bfloat16),
            pltpu.VMEM((DEG, 2, packed, width), jnp.bfloat16),
            pltpu.VMEM((DEG, 4, rows, width), jnp.bfloat16),
            pltpu.VMEM((n_state, packed, width), jnp.bfloat16),
            pltpu.VMEM((n_state, packed, width), jnp.bfloat16),
            pltpu.VMEM((n_state, packed, width), jnp.bfloat16),
            pltpu.VMEM((n_state, packed, width), jnp.bfloat16),
            pltpu.VMEM(blocks.shape, jnp.bfloat16),
            pltpu.VMEM((2, rows, width), jnp.bfloat16),
            pltpu.VMEM((4, 8, width), jnp.int32),
            pltpu.VMEM((4, 8, width), jnp.int32),
            dma,
            dma,
            dma((n_state,)),
            dma((n_state,)),
            dma((DEG, 2)),
            dma((DEG, 2)),
            dma((DEG, 2)),
            dma((DEG, 2)),
            dma((n_state,)),
            dma((n_state,)),
        ],
        compiler_params=pltpu.CompilerParams(
            collective_id=0, has_side_effects=True, vmem_limit_bytes=66000000
        ),
    )(counts, neighbors.T, orbitals.reshape(pair * rows, states), rotation, blocks)


def solution(mesh):
    n_elem, n_state = mesh.shape["elem"], mesh.shape["state"]
    in_specs = (
        P(("elem", "state"), None, None),
        P(),
        P("elem"),
        P("elem", None),
        P("elem", None, None, None),
    )
    return jax.shard_map(
        functools.partial(on_device, n_elem, n_state),
        mesh=mesh,
        in_specs=in_specs,
        out_specs=P(("elem", "state"), None, None),
        check_vma=False,
    )
```

time: 89.4 us -> 79.7 us (0.89)
  Pallas kernels: 84.6 us -> 77.7 us
  local copies, waits for them, and re-layouts: 4.51 us -> 1.84 us
    pallas_call x1, Pallas kernels: 84.6 us -> 77.7 us  [on_device(): pl.pallas_call(functools.partial(kernel, n_elem, n_state), out_shape=jax....]
    unnamed x8 -> x1, local copies, waits for them, and re-layouts: 4.51 us -> 1.84 us
where the time goes in v2:
time: 79.7 us; the launch traced here: 79.5 us
  Pallas kernels  77.7 us (97%)
  local copies, waits for them, and re-layouts  1.84 us (2%)
    pallas_call x1, Pallas kernels, on_device(): pl.pallas_call(functools.partial(kernel, n_elem, n_state), out_shape=jax....  77.7 us
    unnamed x1, local copies, waits for them, and re-layouts  1.84 us

profile of v2, /device:TPU:64, one launch (start us, length us, event | category | flops | bytes accessed | tf_op | source)
XLA Modules:
  0.0 79.5 jit_solution(16804400108785641555)
XLA Ops:
  0.0 77.7 %shard_map.55 = bf16[2,160,768]{2,1,0:T(8,128)(2,1)} custom-call(s32[12]{0:T(128)} %counts_hbm.1, s32[5,12]{1,0:T(8,128)} %bitcast.3, bf16[320,768]{1,0:T(8,128)(2,1)} %bitcast.2, bf16[768,768]{1,0:T(8,128)(2,1)} %rotation_hbm.1, bf16[12,5,160,160]{3,2,1,0:T(8,128)(2,1)} %blocks_hbm.1), custom_call_target="tpu_custom_call" | custom-call | tf_op jit(solution)/shard_map/pallas_call | solution.py:320
  77.7 1.8 %copy.7 = bf16[2,160,768]{2,1,0:T(8,128)(2,1)} copy(bf16[2,160,768]{2,1,0:T(8,128)(2,1)} %shard_map.55) | data formatting | bytes 983040

commit v3 on v2

--- a/solution.py
+++ b/solution.py
@@ -15,7 +15,7 @@
 
 def kernel(
     n_elem, n_state, counts_hbm, neighbors_hbm, orbitals_hbm, rotation_hbm, blocks_hbm, out,
-    counts, neighbors, orbitals, rotation, load_sem, fields, far_out, far_halo, near_halo, last,
+    counts, neighbors, orbitals, rotation, load_sem, column_sem, fields, far_out, far_halo, near_halo, last,
     staged, landed, homed, blocks, scratch, own_counts, far_counts, count_send, count_recv,
     a2a_send, a2a_recv, far_send, far_recv, near_send, near_recv, out_send, out_recv,
 ):
@@ -35,15 +35,25 @@
     far_id = (far, n_state - 1 - spot)
     near_id = (me + 1 - 2 * core, spot)
 
+    def column_load(place):
+        columns = pl.ds(pl.multiple_of(block_at(place) * width, width), width)
+        return pltpu.make_async_copy(
+            rotation_hbm.at[:, columns], rotation.at[:, columns], column_sem.at[place]
+        )
+
+    furthest = jnp.where(spot < n_state // 2, n_state - 1, 0)
     loads = [
         pltpu.make_async_copy(source, target, load_sem.at[i])
         for i, (source, target) in enumerate([
-            (counts_hbm, counts), (orbitals_hbm, orbitals), (rotation_hbm, rotation),
+            (counts_hbm, counts), (orbitals_hbm, orbitals),
             (neighbors_hbm, neighbors), (blocks_hbm, blocks),
         ])
     ]
-    for load in loads:
+    column_load(furthest).start()
+    for load in loads[:2]:
         load.start()
+    for step in range(1, n_state):
+        column_load(lax.rem(furthest + step, n_state)).start()
 
     barrier = pltpu.get_barrier_semaphore()
     for step in range(1, n_state):
@@ -53,7 +63,7 @@
     for device in (far_id, near_id):
         pl.semaphore_signal(barrier, inc=1, device_id=device, device_id_type=MESH)
 
-    for load in loads[:3]:
+    for load in loads[:2]:
         load.wait()
     row = lax.broadcasted_iota(jnp.int32, (rows, width), 0)
     main = 128
@@ -91,14 +101,11 @@
             device_id_type=MESH,
         )
 
-    def place_at(step):
-        return jnp.where(lax.rem(step, 2) == 0, step // 2, n_state - 1 - step // 2)
-
     limits = [counts[2 * spot], counts[2 * spot + 1]]
 
-    def stage(step):
-        place = place_at(step)
+    def stage(place):
         columns = pl.ds(pl.multiple_of(block_at(place) * width, width), width)
+        column_load(place).wait()
         result = jnp.dot(
             orbitals[...], rotation[:, columns], preferred_element_type=jnp.float32
         )
@@ -107,13 +114,6 @@
             for a in range(2)
         ]
         pack(staged.at[place], first, second)
-
-    def send(step):
-        place = place_at(step)
-
-        @pl.when(place != spot)
-        def _():
-            a2a_copy(place).start()
 
     far_own = jnp.where(core == 0, 0, elems - reach)
     for j in range(reach):
@@ -126,15 +126,25 @@
         device_id=far_id,
         device_id_type=MESH,
     )
-    stage(0)
+    stage(furthest)
+    for load in loads[2:]:
+        load.start()
     pl.semaphore_wait(barrier, n_state + 1)
-    send(0)
+    a2a_copy(furthest).start()
     count_copy.start()
 
-    @pl.loop(1, n_state)
+    @pl.loop(1, 2 * n_state - 2)
     def _(step):
-        stage(step)
-        send(step)
+        distance = n_state - 1 - step // 2
+        side = jnp.where(spot < n_state // 2, 1, -1) * (1 - 2 * lax.rem(step, 2))
+        place = spot + side * distance
+
+        @pl.when((place >= 0) & (place < n_state) & (place != furthest))
+        def _():
+            stage(place)
+            a2a_copy(place).start()
+
+    stage(spot)
 
     def arrived(pair):
         @pl.when(pair != spot)
@@ -199,7 +209,7 @@
         arrived(pair)
         settle(pair)
     count_copy.wait()
-    for load in loads[3:]:
+    for load in loads[2:]:
         load.wait()
 
     start_of_all = me * elems - reach
@@ -327,7 +337,8 @@
             pltpu.SMEM(neighbors.shape[::-1], jnp.int32),
             pltpu.VMEM((pair * rows, states), jnp.bfloat16),
             pltpu.VMEM(rotation.shape, jnp.bfloat16),
-            dma((5,)),
+            dma((4,)),
+            dma((n_state,)),
             pltpu.VMEM((DEG, elems + 8, rows, width), jnp.bfloat16),
             pltpu.VMEM((DEG, 2, packed, width), jnp.bfloat16),
             pltpu.VMEM((DEG, 2, packed, width), jnp.bfloat16),
@@ -352,9 +363,12 @@
             dma((n_state,)),
         ],
         compiler_params=pltpu.CompilerParams(
-            collective_id=0, has_side_effects=True, vmem_limit_bytes=66000000
+            collective_id=0, has_side_effects=True, vmem_limit_bytes=48 * 1024 * 1024
         ),
-    )(counts, neighbors.T, orbitals.reshape(pair * rows, states), rotation, blocks)
+    )(*[
+        pltpu.with_memory_space_constraint(x, pltpu.HBM)
+        for x in (counts, neighbors.T, orbitals.reshape(pair * rows, states), rotation, blocks)
+    ])
 
 
 def solution(mesh):

time: 79.7 us -> 78.1 us (0.980)
  local copies, waits for them, and re-layouts: 1.84 us -> 0.78 us
    unnamed x1, local copies, waits for them, and re-layouts: 1.84 us -> 0.78 us
where the time goes in v3:
time: 78.1 us; the launch traced here: 77.9 us
  Pallas kernels  77.2 us (99%)
    pallas_call x1, Pallas kernels, on_device(): pl.pallas_call(functools.partial(kernel, n_elem, n_state), out_shape=jax....  77.2 us

profile of v3, /device:TPU:64, one launch (start us, length us, event | category | flops | bytes accessed | tf_op | source)
XLA Modules:
  0.0 77.9 jit_solution(1878080354581508460)
XLA Ops:
  0.0 77.2 %shard_map.55 = bf16[2,160,768]{2,1,0:T(8,128)(2,1)S(1)} custom-call(s32[12]{0:T(128)} %counts_hbm.1, s32[5,12]{1,0:T(8,128)} %bitcast.3, bf16[320,768]{1,0:T(8,128)(2,1)} %bitcast.2, bf16[768,768]{1,0:T(8,128)(2,1)} %rotation_hbm.1, bf16[12,5,160,160]{3,2,1,0:T(8,128)(2,1)} %blocks_hbm.1), custom_call_target="tpu_custom_call" | custom-call | tf_op jit(solution)/shard_map/pallas_call | solution.py:330
  77.2 0.8 %copy.7 = bf16[2,160,768]{2,1,0:T(8,128)(2,1)} copy(bf16[2,160,768]{2,1,0:T(8,128)(2,1)S(1)} %shard_map.55) | data formatting | bytes 983040

commit v4 on v3

--- a/solution.py
+++ b/solution.py
@@ -195,7 +195,8 @@
             device_id_type=MESH,
         )
 
-    for piece in range(half):
+    outer, inner = core, 1 - core
+    for piece in (inner, outer):
         arrived(far_own // 2 + piece)
         far_copy(0, piece).start()
     for piece in range(half):
@@ -260,6 +261,26 @@
         def _():
             out_copy(pair).start()
 
+    def receive(level, piece):
+        far_copy(level, piece).wait_recv()
+        fields_pair(
+            far_halo.at[level, piece],
+            level,
+            far_slot + 2 * piece,
+            far_counts[2 * piece, 0:1],
+            far_counts[2 * piece + 1, 0:1],
+        )
+
+    def produce(level, piece):
+        pair = far_own // 2 + piece
+        pair_of(level, pair)
+        if level < DEG:
+            slot = reach + 2 * pair
+            pack(far_out.at[level, piece], fields[level, slot], fields[level, slot + 1])
+            far_copy(level, piece).start()
+        else:
+            ship(pair)
+
     for level in range(1, DEG + 1):
         for pair in range(half, elems // 2 - half):
             pair_of(level, pair)
@@ -275,24 +296,16 @@
                 near_copy(level, piece).start()
             else:
                 ship(pair)
-        for piece in range(half):
-            far_copy(level - 1, piece).wait_recv()
-            fields_pair(
-                far_halo.at[level - 1, piece],
-                level - 1,
-                far_slot + 2 * piece,
-                far_counts[2 * piece, 0:1],
-                far_counts[2 * piece + 1, 0:1],
-            )
-        for piece in range(half):
-            pair = far_own // 2 + piece
-            pair_of(level, pair)
-            if level < DEG:
-                slot = reach + 2 * pair
-                pack(far_out.at[level, piece], fields[level, slot], fields[level, slot + 1])
-                far_copy(level, piece).start()
-            else:
-                ship(pair)
+        if level % 2 == 0:
+            receive(level - 1, inner)
+            produce(level, inner)
+            receive(level - 1, outer)
+            produce(level, outer)
+        else:
+            receive(level - 1, outer)
+            receive(level - 1, inner)
+            produce(level, outer)
+            produce(level, inner)
 
     def deliver(source, place):
         columns = pl.ds(pl.multiple_of(block_at(place) * width, width), width)

time: 78.1 us -> 77.5 us (level)
  the two profiles are of different devices: /device:TPU:64 before, /device:TPU:4 now
where the time goes in v4:
time: 77.5 us; the launch traced here: 77.4 us
  Pallas kernels  76.6 us (99%)
  local copies, waits for them, and re-layouts  0.78 us (1%)
    pallas_call x1, Pallas kernels, on_device(): pl.pallas_call(functools.partial(kernel, n_elem, n_state), out_shape=jax....  76.6 us

profile of v4, /device:TPU:4, one launch (start us, length us, event | category | flops | bytes accessed | tf_op | source)
XLA Modules:
  0.0 77.4 jit_solution(11687289477488068758)
XLA Ops:
  0.0 76.6 %shard_map.55 = bf16[2,160,768]{2,1,0:T(8,128)(2,1)S(1)} custom-call(s32[12]{0:T(128)} %counts_hbm.1, s32[5,12]{1,0:T(8,128)} %bitcast.3, bf16[320,768]{1,0:T(8,128)(2,1)} %bitcast.2, bf16[768,768]{1,0:T(8,128)(2,1)} %rotation_hbm.1, bf16[12,5,160,160]{3,2,1,0:T(8,128)(2,1)} %blocks_hbm.1), custom_call_target="tpu_custom_call" | custom-call | tf_op jit(solution)/shard_map/pallas_call | solution.py:343
  76.6 0.8 %copy.7 = bf16[2,160,768]{2,1,0:T(8,128)(2,1)} copy(bf16[2,160,768]{2,1,0:T(8,128)(2,1)S(1)} %shard_map.55) | data formatting | bytes 983040

commit v5 on v4

--- a/solution.py
+++ b/solution.py
@@ -282,10 +282,6 @@
             ship(pair)
 
     for level in range(1, DEG + 1):
-        for pair in range(half, elems // 2 - half):
-            pair_of(level, pair)
-            if level == DEG:
-                ship(pair)
         for piece in range(half):
             near_copy(level - 1, piece).wait_recv()
         fields[level - 1, pl.ds(near_slot, reach)] = near_halo[level - 1]
@@ -295,6 +291,10 @@
             if level < DEG:
                 near_copy(level, piece).start()
             else:
+                ship(pair)
+        for pair in range(half, elems // 2 - half):
+            pair_of(level, pair)
+            if level == DEG:
                 ship(pair)
         if level % 2 == 0:
             receive(level - 1, inner)

time: 77.5 us -> 77.4 us (level)
  the two profiles are of different devices: /device:TPU:4 before, /device:TPU:6 now
where the time goes in v5:
time: 77.4 us; the launch traced here: 77.2 us
  Pallas kernels  76.4 us (99%)
  local copies, waits for them, and re-layouts  0.78 us (1%)
    pallas_call x1, Pallas kernels, on_device(): pl.pallas_call(functools.partial(kernel, n_elem, n_state), out_shape=jax....  76.4 us

profile of v5, /device:TPU:6, one launch (start us, length us, event | category | flops | bytes accessed | tf_op | source)
XLA Modules:
  0.0 77.2 jit_solution(8182316052134414817)
XLA Ops:
  0.0 76.4 %shard_map.55 = bf16[2,160,768]{2,1,0:T(8,128)(2,1)S(1)} custom-call(s32[12]{0:T(128)} %counts_hbm.1, s32[5,12]{1,0:T(8,128)} %bitcast.3, bf16[320,768]{1,0:T(8,128)(2,1)} %bitcast.2, bf16[768,768]{1,0:T(8,128)(2,1)} %rotation_hbm.1, bf16[12,5,160,160]{3,2,1,0:T(8,128)(2,1)} %blocks_hbm.1), custom_call_target="tpu_custom_call" | custom-call | tf_op jit(solution)/shard_map/pallas_call | solution.py:343
  76.4 0.8 %copy.7 = bf16[2,160,768]{2,1,0:T(8,128)(2,1)} copy(bf16[2,160,768]{2,1,0:T(8,128)(2,1)S(1)} %shard_map.55) | data formatting | bytes 983040

commit v6 on v4

--- a/solution.py
+++ b/solution.py
@@ -235,14 +235,13 @@
 
     def pair_of(level, pair):
         if level < DEG:
-            @pl.loop(0, 2)
-            def _(a):
-                e = 2 * pair + a
-                fields[level, reach + e] = updated(level, e)
+            values = [updated(level, 2 * pair + a) for a in range(2)]
+            for a in range(2):
+                fields[level, reach + 2 * pair + a] = values[a]
         else:
-            @pl.loop(0, 2)
-            def _(a):
-                scratch[a] = updated(level, 2 * pair + a)
+            values = [updated(level, 2 * pair + a) for a in range(2)]
+            for a in range(2):
+                scratch[a] = values[a]
 
             pack(last.at[pair], scratch[0], scratch[1])
 

time: 77.5 us -> 77.1 us (level)
  the two profiles are of different devices: /device:TPU:4 before, /device:TPU:6 now
where the time goes in v6:
time: 77.1 us; the launch traced here: 77 us
  Pallas kernels  76.2 us (99%)
  local copies, waits for them, and re-layouts  0.78 us (1%)
    pallas_call x1, Pallas kernels, on_device(): pl.pallas_call(functools.partial(kernel, n_elem, n_state), out_shape=jax....  76.2 us

profile of v6, /device:TPU:6, one launch (start us, length us, event | category | flops | bytes accessed | tf_op | source)
XLA Modules:
  0.0 77.0 jit_solution(17912492446600057525)
XLA Ops:
  0.0 76.2 %shard_map.55 = bf16[2,160,768]{2,1,0:T(8,128)(2,1)S(1)} custom-call(s32[12]{0:T(128)} %counts_hbm.1, s32[5,12]{1,0:T(8,128)} %bitcast.3, bf16[320,768]{1,0:T(8,128)(2,1)} %bitcast.2, bf16[768,768]{1,0:T(8,128)(2,1)} %rotation_hbm.1, bf16[12,5,160,160]{3,2,1,0:T(8,128)(2,1)} %blocks_hbm.1), custom_call_target="tpu_custom_call" | custom-call | tf_op jit(solution)/shard_map/pallas_call | solution.py:342
  76.2 0.8 %copy.7 = bf16[2,160,768]{2,1,0:T(8,128)(2,1)} copy(bf16[2,160,768]{2,1,0:T(8,128)(2,1)S(1)} %shard_map.55) | data formatting | bytes 983040

commit v7 on v4

--- a/solution.py
+++ b/solution.py
@@ -289,7 +289,7 @@
         for piece in range(half):
             near_copy(level - 1, piece).wait_recv()
         fields[level - 1, pl.ds(near_slot, reach)] = near_halo[level - 1]
-        for piece in range(half):
+        for piece in (inner, outer):
             pair = near_own // 2 + piece
             pair_of(level, pair)
             if level < DEG:

time: 77.5 us -> 77.5 us (level)
  no operation moved by 1% of the time
where the time goes in v7:
time: 77.5 us; the launch traced here: 77.4 us
  Pallas kernels  76.6 us (99%)
  local copies, waits for them, and re-layouts  0.78 us (1%)
    pallas_call x1, Pallas kernels, on_device(): pl.pallas_call(functools.partial(kernel, n_elem, n_state), out_shape=jax....  76.6 us

profile of v7, /device:TPU:4, one launch (start us, length us, event | category | flops | bytes accessed | tf_op | source)
XLA Modules:
  0.0 77.4 jit_solution(7000389886295402610)
XLA Ops:
  0.0 76.6 %shard_map.55 = bf16[2,160,768]{2,1,0:T(8,128)(2,1)S(1)} custom-call(s32[12]{0:T(128)} %counts_hbm.1, s32[5,12]{1,0:T(8,128)} %bitcast.3, bf16[320,768]{1,0:T(8,128)(2,1)} %bitcast.2, bf16[768,768]{1,0:T(8,128)(2,1)} %rotation_hbm.1, bf16[12,5,160,160]{3,2,1,0:T(8,128)(2,1)} %blocks_hbm.1), custom_call_target="tpu_custom_call" | custom-call | tf_op jit(solution)/shard_map/pallas_call | solution.py:343
  76.6 0.8 %copy.7 = bf16[2,160,768]{2,1,0:T(8,128)(2,1)} copy(bf16[2,160,768]{2,1,0:T(8,128)(2,1)S(1)} %shard_map.55) | data formatting | bytes 983040
